TPU v7x, 32 devices: a whole 2x2x4 slice. The times are simulated.
32 devices in a mesh: img: 2 (over y), cls: 4 (over z), emb: 4 (over x, core).
Axes of the slice: x: 2, y: 2, z: 4, core: 2. Of those that a mesh axis runs over, the one named last changes fastest.
Arguments:
- regions: bfloat16 [2048, 1024], P('img', 'emb'), may hold values from -8 to 8
- table: bfloat16 [21504, 1024], P('cls', 'emb'), may hold values from -1 to 1
- shift: float32 [2048], P('img'), may hold values from -0.5 to 0.1
- scale: float32 [2048], P('img'), may hold values from 2 to 20
- labels: int32 [2048], P('img'), may hold values from -1 to 21503, as said below
- valid: int32 [4, 21504], P('img', 'cls'), may hold values 0 or 1
Outputs:
- loss: float32 [], replicated
- region_grad: bfloat16 [2048, 1024], P('img', 'emb')
- table_grad: bfloat16 [21504, 1024], P('cls', 'emb')
Inputs may be any that keep to these rules, and one draw needn't show every extreme that they name: `labels`: -1 marks background; the first region of every image is foreground.
All inputs are finite; a program needn't handle non-finite values. No bound on the sum of `valid` on one device may be relied on, other than what follows from the above.
Results may differ from a plain program's by a relative error of at most 0.0034.
Values may be sent and summed in bfloat16 or wider, within the bound.
A program may use at most 64 MiB of HBM per device.

v0:
```python
import jax
import jax.numpy as jnp
from jax import lax
from jax.sharding import PartitionSpec as P

CLASSES = 21504
REG_IMG = 512


def focal(logit, target):
    prob = jax.nn.sigmoid(logit)
    return -0.25 * target * (1.0 - prob) ** 2 * jax.nn.log_sigmoid(logit) - 0.75 * (
        1.0 - target
    ) * prob**2 * jax.nn.log_sigmoid(-logit)


def shards(regions, table, shift, scale, labels, valid):
    rows = regions.shape[0]
    class_dev = table.shape[0]
    parts = lax.axis_size("emb")
    quarter = rows // parts
    start = lax.axis_index("emb") * quarter
    block = regions.astype(jnp.float32)
    squares = lax.psum(jnp.sum(block * block, axis=1), "emb")
    local_count = jnp.sum((labels >= 0).astype(jnp.float32))
    count = lax.psum(local_count, "img")
    inv = lax.rsqrt(squares + 1e-06)
    unit = block * inv[:, None]
    unit_b = unit.astype(jnp.bfloat16)
    unit_rows = lax.all_to_all(unit_b, "emb", split_axis=0, concat_axis=1, tiled=True)
    cosine = lax.dot_general(
        unit_rows,
        lax.all_gather(table, "emb", axis=1, tiled=True),
        (((1,), (1,)), ((), ())),
        preferred_element_type=jnp.float32,
    )
    shift_q = lax.dynamic_slice_in_dim(shift, start, quarter, 0)
    scale_q = lax.dynamic_slice_in_dim(scale, start, quarter, 0)
    label_q = lax.dynamic_slice_in_dim(labels, start, quarter, 0)
    image_ids = (start + jnp.arange(quarter, dtype=jnp.int32)) // REG_IMG
    onehot = (image_ids[:, None] == jnp.arange(valid.shape[0], dtype=jnp.int32)[None, :]).astype(
        jnp.float32
    )
    mask = jnp.dot(onehot, valid.astype(jnp.float32), preferred_element_type=jnp.float32)
    class_ids = lax.axis_index("cls") * class_dev + jnp.arange(class_dev, dtype=jnp.int32)
    logit = (cosine + shift_q[:, None]) * scale_q[:, None]
    target = (label_q[:, None] == class_ids[None, :]).astype(jnp.float32)
    term, pullback = jax.vjp(lambda value: focal(value, target), logit)
    dlogit = pullback(jnp.ones_like(term))[0]
    total = lax.psum(jnp.sum(term * mask), ("img", "cls", "emb"))
    factor = rows * lax.axis_size("img") / count
    dscore = (dlogit * mask * scale_q[:, None] * factor).astype(jnp.bfloat16)
    piece = lax.all_gather(dscore, "emb", axis=0, tiled=True)
    dunit_piece = jnp.dot(piece, table, preferred_element_type=jnp.float32)
    table_acc = lax.dot_general(
        piece, unit_b, (((0,), (0,)), ((), ())), preferred_element_type=jnp.float32
    )
    dunit = lax.psum(dunit_piece, "cls")
    radial = lax.psum(jnp.sum(unit * dunit, axis=1), "emb")
    region_grad = (inv[:, None] * (dunit - unit * radial[:, None])).astype(jnp.bfloat16)
    table_grad = lax.psum(table_acc, "img").astype(jnp.bfloat16)
    loss = total / count / CLASSES
    return (loss, region_grad, table_grad)


def solution(mesh):
    placed = (P("img", "emb"), P("cls", "emb"), P("img"), P("img"), P("img"), P("img", "cls"))
    return jax.shard_map(
        shards,
        mesh=mesh,
        in_specs=placed,
        out_specs=(P(), P("img", "emb"), P("cls", "emb")),
        check_vma=False,
    )
```

profile of v0, /device:TPU:0, one launch (start us, length us, event | category | flops | bytes accessed | tf_op | source)
XLA Modules:
  0.0 357.9 jit_solution(13751728279272978331)
XLA Ops:
  7.2 0.0 copy-start.2
  7.2 0.0 all-gather.3.cloned.1.call-start
  7.2 0.7 all-gather.3.cloned.1.call-update
  7.9 1.3 fusion.33
  9.2 8.4 %psum.42 = f32[1024]{0:T(1024)S(1)} all-reduce(f32[1024]{0:T(1024)S(1)} %fusion.33), channel_id=1, replica_groups=mesh['img'=2,'cls'=4,'emb'=4] {'emb'}, use_global_device_ids=true, to_apply=%region_1.0 | all-reduce | flops 1024 | bytes 8192 | tf_op jit(solution)/shard_map/psum | solution.py:24
  17.6 1.3 fusion.28
  18.9 1.0 copy.9
  19.9 3.5 all-to-all-start
  23.4 0.0 all-gather.5.cloned.1.call-start
  23.5 0.0 copy-done.2
  23.5 0.6 convert_reduce_fusion
  24.1 5.5 %psum.44 = f32[]{:T(128)} all-reduce(f32[]{:T(128)} %convert_reduce_fusion), channel_id=1, replica_groups=mesh['img'=2,'cls'=4,'emb'=4] {'img'}, use_global_device_ids=true, to_apply=%region_5.7 | all-reduce | flops 1 | bytes 8 | tf_op jit(solution)/shard_map/psum | solution.py:26
  29.6 0.1 dynamic_slice.9
  29.7 0.8 dynamic_slice.11
  30.5 0.8 dynamic_slice.10
  31.9 6.3 %all-to-all-done = bf16[4,256,256]{1,2,0:T(8,128)(2,1)S(1)} async-done(((bf16[4,256,256]{1,2,0:T(8,128)(2,1)}), bf16[4,256,256]{1,2,0:T(8,128)(2,1)S(1)}, u32[]{:S(2)}, u32[]{:S(2)}) %all-to-all-start) | async-done | bytes 524320 | tf_op jit(solution)/shard_map/all_to_all | solution.py:30
  38.2 54.3 %all-gather.3.cloned.1.call-done = bf16[5376,1024]{1,0:T(8,128)(2,1)} async-done(((bf16[5376,256]{1,0:T(8,128)(2,1)}), bf16[5376,1024]{1,0:T(8,128)(2,1)}) %all-gather.3.cloned.1.call-update) | async-done | bytes 11010064 | tf_op jit(solution)/shard_map/all_gather | solution.py:33
  92.5 6.5 %fusion = f32[256,5376]{1,0:T(8,128)S(1)} fusion(bf16[256,1024]{0,1:T(8,128)(2,1)S(1)} %bitcast.11, bf16[5376,1024]{1,0:T(8,128)(2,1)} %all-gather.3.cloned.1.call-done, f32[256]{0:T(256)S(1)} %dynamic_slice.11, f32[256]{0:T(256)S(1)} %dynamic_slice.10), kind=kOutput, calls=%fused_computation.7 | convolution fusion | flops 2821324800 | bytes 17041408 | tf_op jit(solution)/shard_map/dot_general | solution.py:31
  99.1 0.0 copy-start.1
  99.1 18.2 %fusion.12 = (bf16[256,5376]{1,0:T(8,128)(2,1)}, f32[]{:T(128)}) fusion(f32[256,5376]{1,0:T(8,128)S(1)} %fusion, f32[]{:T(128)S(6)} %div.31, f32[256]{0:T(256)S(1)} %dynamic_slice.11, s32[5376]{0:T(1024)S(1)} %iota_add_fusion, s32[256]{0:T(256)S(1)} %dynamic_slice.9, s32[2,5376]{1,0:T(2,128)S(1)} %copy-done.3, s32[256]{0:T(256)S(1)} %and_select_fusion), kind=kOutput, calls=%fused_computation.25 | convolution fusion | flops 94972928 | bytes 8325128 | tf_op jit(solution)/shard_map/dot_general | solution.py:44
  117.3 0.0 all-gather.5.cloned.1.call-update
  117.3 0.0 all-reduce.3.cloned.1.call-start
  117.4 40.5 %psum.43 = f32[]{:T(128)} all-reduce(f32[]{:T(128)} %get-tuple-element.12), channel_id=1, replica_groups=mesh['img'=2,'cls'=4,'emb'=4] {'img','cls','emb'}, use_global_device_ids=true, to_apply=%region_3.5 | all-reduce | flops 1 | bytes 8 | tf_op jit(solution)/shard_map/psum | solution.py:50
  159.2 32.3 %all-gather.5.cloned.1.call-done = bf16[1024,5376]{1,0:T(8,128)(2,1)} async-done(((bf16[256,5376]{1,0:T(8,128)(2,1)}), bf16[1024,5376]{1,0:T(8,128)(2,1)}) %all-gather.5.cloned.1.call-update) | async-done | bytes 11010064 | tf_op jit(solution)/shard_map/all_gather | solution.py:53
  191.5 8.1 %fusion.37 = f32[1024,256]{1,0:T(8,128)} fusion(bf16[1024,5376]{1,0:T(8,128)(2,1)} %all-gather.5.cloned.1.call-done, bf16[5376,256]{1,0:T(8,128)(2,1)S(1)} %copy-done.1), kind=kOutput, calls=%fused_computation.63 | convolution fusion | flops 2818572288 | bytes 14811136 | tf_op jit(solution)/shard_map/dot_general | solution.py:54
  199.6 0.0 all-reduce.3.cloned.1.call-update
  199.7 9.6 %fusion.38 = f32[5376,256]{1,0:T(8,128)} fusion(bf16[1024,5376]{1,0:T(8,128)(2,1)} %all-gather.5.cloned.1.call-done, bf16[1024,256]{1,0:T(8,128)(2,1)S(1)} %fusion.28), kind=kOutput, calls=%fused_computation.64 | convolution fusion | flops 2818572288 | bytes 17039360 | tf_op jit(solution)/shard_map/dot_general | solution.py:55
  209.2 131.1 %all-reduce.4 = bf16[5376,256]{1,0:T(8,128)(2,1)} all-reduce(f32[5376,256]{1,0:T(8,128)} %fusion.38), channel_id=1, replica_groups=mesh['img'=2,'cls'=4,'emb'=4] {'img'}, use_global_device_ids=true, to_apply=%region_9.11 | all-reduce | flops 1376256 | bytes 8257536 | tf_op jit(solution)/shard_map/psum | solution.py:61
  340.4 0.0 copy-done
  340.4 1.6 fusion.29
  342.0 5.9 %psum.46 = f32[1024]{0:T(1024)S(1)} all-reduce(f32[1024]{0:T(1024)S(1)} %fusion.29), channel_id=1, replica_groups=mesh['img'=2,'cls'=4,'emb'=4] {'emb'}, use_global_device_ids=true, to_apply=%region_8.10 | all-reduce | flops 1024 | bytes 8192 | tf_op jit(solution)/shard_map/psum | solution.py:59
  347.9 2.4 fusion.32
  (8 shorter events, 0.0 us)
Async XLA Ops:
  7.2 16.3 %copy-start.2 = (s32[1024]{0:T(1024)S(1)}, s32[1024]{0:T(1024)}, u32[]{:S(2)}) copy-start(s32[1024]{0:T(1024)} %param.11) | copy-start | bytes 12292
  7.2 85.4 %all-gather.3.cloned.1.call-start = ((), (), s32[]{:S(2)}) async-start(), calls=%async_computation.1 | async-start | bytes 13762560 | tf_op jit(solution)/shard_map/all_gather | solution.py:33
  19.9 18.4 %all-to-all-start = ((bf16[4,256,256]{1,2,0:T(8,128)(2,1)}), bf16[4,256,256]{1,2,0:T(8,128)(2,1)S(1)}, u32[]{:S(2)}, u32[]{:S(2)}) async-start(bf16[4,256,256]{1,2,0:T(8,128)(2,1)} %copy.9), calls=%async_computation | async-start | bytes 1048576 | tf_op jit(solution)/shard_map/all_to_all | solution.py:30
  23.4 168.1 %all-gather.5.cloned.1.call-start = ((), (), s32[]{:S(2)}) async-start(), calls=%async_computation.2 | async-start | bytes 13762560 | tf_op jit(solution)/shard_map/all_gather | solution.py:53
  92.5 6.5 %copy-start.3 = (s32[2,5376]{1,0:T(2,128)S(1)}, s32[2,5376]{1,0:T(2,128)}, u32[]{:S(2)}) copy-start(s32[2,5376]{1,0:T(2,128)} %param.12) | copy-start | bytes 129028
  99.1 92.4 %copy-start.1 = (bf16[5376,256]{1,0:T(8,128)(2,1)S(1)}, bf16[5376,256]{1,0:T(8,128)(2,1)}, u32[]{:S(2)}) copy-start(bf16[5376,256]{1,0:T(8,128)(2,1)} %param.8) | copy-start | bytes 8257540
  117.3 223.1 %all-reduce.3.cloned.1.call-start = ((), (), s32[]{:S(2)}) async-start(), calls=%async_computation.3 | async-start | bytes 2097152 | tf_op jit(solution)/shard_map/psum | solution.py:58
  209.2 131.2 %copy-start = (bf16[1024,256]{1,0:T(8,128)(2,1)S(1)}, bf16[1024,256]{1,0:T(8,128)(2,1)}, u32[]{:S(2)}) copy-start(bf16[1024,256]{1,0:T(8,128)(2,1)} %param.7) | copy-start | bytes 1572868
Sparse Core Ops, SparseCore 0:
  9.5 82.9 all-gather.2
  117.4 74.0 all-gather.4
  199.8 51.7 all-reduce.2
where the time goes:
time: 359 us; the launch traced here: 358 us
  blocking collectives  191 us (53%)
  waiting for transfers between devices  93.6 us (26%)
  matrix products  42.4 us (12%)
  between operations  17 us (5%)
  other arithmetic  7.16 us (2%)
  starting transfers between devices  3.66 us (1%)
    psum x1, blocking collectives, shards(): table_grad = lax.psum(table_acc, 'img').astype(jnp.bfloat16)  131 us
    all_gather x1, waiting for transfers between devices, shards(): lax.all_gather(table, 'emb', axis=1, tiled=True)  54.3 us
    psum x1, blocking collectives, shards(): total = lax.psum(jnp.sum(term * mask), ('img', 'cls', 'emb'))  40.5 us
    all_gather x1, waiting for transfers between devices, shards(): piece = lax.all_gather(dscore, 'emb', axis=0, tiled=True)  32.3 us
    dot_general x1, matrix products, shards(): jnp.dot(onehot, valid.astype(jnp.float32), preferred_element_type=jnp.flo...  18.2 us
    dot_general x1, matrix products, shards(): lax.dot_general(piece, unit_b, (((0,), (0,)), ((), ())), preferred_elemen...  9.56 us
    psum x1, blocking collectives, shards(): squares = lax.psum(jnp.sum(block * block, axis=1), 'emb')  8.38 us
    dot_general x1, matrix products, shards(): dunit_piece = jnp.dot(piece, table, preferred_element_type=jnp.float32)  8.13 us
  transfers between devices with their start and end apart: 4, of which 3 were waited for; matrix products, arithmetic and copies ran while one was open for 4% of the time, Pallas kernels for 0%

commit v1 on v0

--- a/solution.py
+++ b/solution.py
@@ -5,6 +5,11 @@
 
 CLASSES = 21504
 REG_IMG = 512
+
+
+def _perform_corner(row_data, net_axis, d0):
+    state_next = jnp.concatenate(lax.all_gather(row_data, net_axis), axis=d0)
+    return state_next
 
 
 def focal(logit, target):
@@ -30,7 +35,7 @@
     unit_rows = lax.all_to_all(unit_b, "emb", split_axis=0, concat_axis=1, tiled=True)
     cosine = lax.dot_general(
         unit_rows,
-        lax.all_gather(table, "emb", axis=1, tiled=True),
+        _perform_corner(table, "emb", 1),
         (((1,), (1,)), ((), ())),
         preferred_element_type=jnp.float32,
     )

time: 359 us -> 357 us (level)
  transfers between devices with their start and end apart: 4 -> 4, of which waited for: 3 -> 3; matrix products, arithmetic and copies ran while one was open for 4% -> 5% of each run, Pallas kernels for 0% -> 0%
where the time goes in v1:
time: 357 us; the launch traced here: 356 us
  blocking collectives  191 us (54%)
  waiting for transfers between devices  91.2 us (26%)
  matrix products  41.9 us (12%)
  between operations  16.9 us (5%)
  other arithmetic  8.66 us (2%)
  starting transfers between devices  3.61 us (1%)
    psum x1, blocking collectives, shards(): table_grad = lax.psum(table_acc, 'img').astype(jnp.bfloat16)  131 us
    all_gather x1, waiting for transfers between devices, _perform_corner(): state_next = jnp.concatenate(lax.all_gather(row_data, net_axis), axis=d0)  53.1 us
    psum x1, blocking collectives, shards(): total = lax.psum(jnp.sum(term * mask), ('img', 'cls', 'emb'))  40.4 us
    all_gather x1, waiting for transfers between devices, shards(): piece = lax.all_gather(dscore, 'emb', axis=0, tiled=True)  32.5 us
    dot_general x1, matrix products, shards(): jnp.dot(onehot, valid.astype(jnp.float32), preferred_element_type=jnp.flo...  18.2 us
    dot_general x1, matrix products, shards(): lax.dot_general(piece, unit_b, (((0,), (0,)), ((), ())), preferred_elemen...  9.6 us
    psum x1, blocking collectives, shards(): squares = lax.psum(jnp.sum(block * block, axis=1), 'emb')  8.38 us
    dot_general x1, matrix products, shards(): dunit_piece = jnp.dot(piece, table, preferred_element_type=jnp.float32)  8.13 us
  transfers between devices with their start and end apart: 4, of which 3 were waited for; matrix products, arithmetic and copies ran while one was open for 5% of the time, Pallas kernels for 0%

profile of v1, /device:TPU:0, one launch (start us, length us, event | category | flops | bytes accessed | tf_op | source)
XLA Modules:
  0.0 355.9 jit_solution(14972819573240790919)
XLA Ops:
  7.2 0.0 all-gather.6.cloned.1.call-start
  7.2 0.7 all-gather.6.cloned.1.call-update
  7.9 1.3 fusion.34
  9.2 8.4 %psum.42 = f32[1024]{0:T(1024)S(1)} all-reduce(f32[1024]{0:T(1024)S(1)} %fusion.34), channel_id=1, replica_groups=mesh['img'=2,'cls'=4,'emb'=4] {'emb'}, use_global_device_ids=true, to_apply=%region_1.0 | all-reduce | flops 1024 | bytes 8192 | tf_op jit(solution)/shard_map/psum | solution.py:29
  17.5 2.1 fusion.29
  19.7 3.5 all-to-all-start
  23.2 0.0 all-gather.4.cloned.1.call-start
  23.2 1.3 convert_reduce_fusion
  24.5 5.5 %psum.44 = f32[]{:T(128)} all-reduce(f32[]{:T(128)} %convert_reduce_fusion), channel_id=1, replica_groups=mesh['img'=2,'cls'=4,'emb'=4] {'img'}, use_global_device_ids=true, to_apply=%region_5.7 | all-reduce | flops 1 | bytes 8 | tf_op jit(solution)/shard_map/psum | solution.py:31
  30.0 0.8 dynamic_slice.9
  30.8 0.8 dynamic_slice.11
  31.6 0.8 dynamic_slice.10
  33.0 4.9 %all-to-all-done = bf16[4,256,256]{2,1,0:T(8,128)(2,1)S(1)} async-done(((bf16[4,256,256]{2,1,0:T(8,128)(2,1)}), bf16[4,256,256]{2,1,0:T(8,128)(2,1)S(1)}, u32[]{:S(2)}, u32[]{:S(2)}) %all-to-all-start) | async-done | bytes 524320 | tf_op jit(solution)/shard_map/all_to_all | solution.py:35
  38.0 53.1 %all-gather.6.cloned.1.call-done = bf16[21504,256]{1,0:T(8,128)(2,1)} async-done(((bf16[5376,256]{1,0:T(8,128)(2,1)}), bf16[21504,256]{1,0:T(8,128)(2,1)}) %all-gather.6.cloned.1.call-update) | async-done | bytes 11010064 | tf_op jit(solution)/shard_map/all_gather | solution.py:11
  91.1 0.0 copy-start.2
  91.1 6.0 %fusion.1 = f32[256,5376]{1,0:T(8,128)S(1)} fusion(bf16[5376,4,256]{2,0,1:T(8,128)(2,1)} %bitcast.18, f32[256]{0:T(256)S(1)} %dynamic_slice.11, f32[256]{0:T(256)S(1)} %dynamic_slice.10, bf16[4,256,256]{2,1,0:T(8,128)(2,1)S(1)} %all-to-all-done), kind=kOutput, calls=%fused_computation.8 | convolution fusion | flops 2821324800 | bytes 17041408 | tf_op jit(solution)/shard_map/dot_general | solution.py:36
  97.0 0.0 copy-done.2
  97.1 0.0 copy-start.1
  97.1 18.2 %fusion.13 = (bf16[256,5376]{1,0:T(8,128)(2,1)}, f32[]{:T(128)}) fusion(f32[256,5376]{1,0:T(8,128)S(1)} %fusion.1, f32[]{:T(128)S(6)} %div.31, f32[256]{0:T(256)S(1)} %dynamic_slice.11, s32[5376]{0:T(1024)S(1)} %iota_add_fusion, s32[256]{0:T(256)S(1)} %dynamic_slice.9, s32[2,5376]{1,0:T(2,128)S(1)} %copy-done.2, s32[256]{0:T(256)S(1)} %and_select_fusion), kind=kOutput, calls=%fused_computation.26 | convolution fusion | flops 94972928 | bytes 8325128 | tf_op jit(solution)/shard_map/dot_general | solution.py:49
  115.2 0.0 all-gather.4.cloned.1.call-update
  115.3 0.0 all-reduce.3.cloned.1.call-start
  115.3 40.4 %psum.43 = f32[]{:T(128)} all-reduce(f32[]{:T(128)} %get-tuple-element.12), channel_id=1, replica_groups=mesh['img'=2,'cls'=4,'emb'=4] {'img','cls','emb'}, use_global_device_ids=true, to_apply=%region_3.5 | all-reduce | flops 1 | bytes 8 | tf_op jit(solution)/shard_map/psum | solution.py:55
  157.0 32.5 %all-gather.4.cloned.1.call-done = bf16[1024,5376]{1,0:T(8,128)(2,1)} async-done(((bf16[256,5376]{1,0:T(8,128)(2,1)}), bf16[1024,5376]{1,0:T(8,128)(2,1)}) %all-gather.4.cloned.1.call-update) | async-done | bytes 11010064 | tf_op jit(solution)/shard_map/all_gather | solution.py:58
  189.4 0.0 copy-done.1
  189.4 8.1 %fusion.39 = f32[1024,256]{1,0:T(8,128)} fusion(bf16[1024,5376]{1,0:T(8,128)(2,1)} %all-gather.4.cloned.1.call-done, bf16[5376,256]{1,0:T(8,128)(2,1)S(1)} %copy-done.1), kind=kOutput, calls=%fused_computation.65 | convolution fusion | flops 2818572288 | bytes 14811136 | tf_op jit(solution)/shard_map/dot_general | solution.py:59
  197.6 0.0 all-reduce.3.cloned.1.call-update
  197.6 9.6 %fusion.40 = f32[5376,256]{1,0:T(8,128)} fusion(bf16[1024,5376]{1,0:T(8,128)(2,1)} %all-gather.4.cloned.1.call-done, bf16[1024,256]{1,0:T(8,128)(2,1)} %fusion.29), kind=kOutput, calls=%fused_computation.66 | convolution fusion | flops 2818572288 | bytes 17039360 | tf_op jit(solution)/shard_map/dot_general | solution.py:60
  207.2 131.1 %all-reduce.4 = bf16[5376,256]{1,0:T(8,128)(2,1)} all-reduce(f32[5376,256]{1,0:T(8,128)} %fusion.40), channel_id=1, replica_groups=mesh['img'=2,'cls'=4,'emb'=4] {'img'}, use_global_device_ids=true, to_apply=%region_9.11 | all-reduce | flops 1376256 | bytes 8257536 | tf_op jit(solution)/shard_map/psum | solution.py:66
  338.4 0.0 copy-done
  338.4 1.6 fusion.30
  340.0 5.9 %psum.46 = f32[1024]{0:T(1024)S(1)} all-reduce(f32[1024]{0:T(1024)S(1)} %fusion.30), channel_id=1, replica_groups=mesh['img'=2,'cls'=4,'emb'=4] {'emb'}, use_global_device_ids=true, to_apply=%region_8.10 | all-reduce | flops 1024 | bytes 8192 | tf_op jit(solution)/shard_map/psum | solution.py:64
  345.9 2.4 fusion.33
  (5 shorter events, 0.0 us)
Async XLA Ops:
  7.2 83.9 %all-gather.6.cloned.1.call-start = ((), (), s32[]{:S(2)}) async-start(), calls=%async_computation.3 | async-start | bytes 13762560 | tf_op jit(solution)/shard_map/all_gather | solution.py:11
  19.7 18.3 %all-to-all-start = ((bf16[4,256,256]{2,1,0:T(8,128)(2,1)}), bf16[4,256,256]{2,1,0:T(8,128)(2,1)S(1)}, u32[]{:S(2)}, u32[]{:S(2)}) async-start(bf16[4,256,256]{2,1,0:T(8,128)(2,1)} %bitcast), calls=%async_computation | async-start | bytes 1048576 | tf_op jit(solution)/shard_map/all_to_all | solution.py:35
  23.2 166.3 %all-gather.4.cloned.1.call-start = ((), (), s32[]{:S(2)}) async-start(), calls=%async_computation.1 | async-start | bytes 13762560 | tf_op jit(solution)/shard_map/all_gather | solution.py:58
  91.1 6.0 %copy-start.2 = (s32[2,5376]{1,0:T(2,128)S(1)}, s32[2,5376]{1,0:T(2,128)}, u32[]{:S(2)}) copy-start(s32[2,5376]{1,0:T(2,128)} %param.12) | copy-start | bytes 129028
  97.1 92.4 %copy-start.1 = (bf16[5376,256]{1,0:T(8,128)(2,1)S(1)}, bf16[5376,256]{1,0:T(8,128)(2,1)}, u32[]{:S(2)}) copy-start(bf16[5376,256]{1,0:T(8,128)(2,1)} %param.8) | copy-start | bytes 8257540
  115.3 223.1 %all-reduce.3.cloned.1.call-start = ((), (), s32[]{:S(2)}) async-start(), calls=%async_computation.2 | async-start | bytes 2097152 | tf_op jit(solution)/shard_map/psum | solution.py:63
  207.2 131.2 %copy-start = (bf16[1024,256]{1,0:T(8,128)(2,1)S(1)}, bf16[1024,256]{1,0:T(8,128)(2,1)}, u32[]{:S(2)}) copy-start(bf16[1024,256]{1,0:T(8,128)(2,1)} %param.7) | copy-start | bytes 1572868
Sparse Core Ops, SparseCore 0:
  9.5 81.4 all-gather.5
  115.4 74.0 all-gather.3
  197.7 51.7 all-reduce.2
